TPU v7x, 32 devices: a whole 2x2x4 slice. The times are simulated.
32 devices in a mesh: dp: 2 (over core), blk: 4 (over y, x), rep: 4 (over z).
Axes of the slice: x: 2, y: 2, z: 4, core: 2. Of those that a mesh axis runs over, the one named last changes fastest.
Arguments:
- feats: bfloat16 [2, 16384, 512], P('dp', ('blk', 'rep')), may hold values from -6 to 6
- weight: bfloat16 [512, 512], replicated, may hold values from -0.25 to 0.25
- cols: int32 [2, 128, 15], P('dp', ('blk', 'rep')), may hold values from -1 to 127, as said below
- vals: bfloat16 [2, 128, 15, 128, 128], P('dp', ('blk', 'rep')), as said below
- cotangent: bfloat16 [2, 16384, 512], P('dp', ('blk', 'rep')), may hold values from -6 to 6
Outputs:
- activ: bfloat16 [2, 16384, 512], P('dp', ('blk', 'rep'))
- feat_grad: bfloat16 [2, 16384, 512], P('dp', ('blk', 'rep'))
- weight_grad: float32 [512, 512], replicated
Inputs may be any that keep to these rules, and one draw needn't show every extreme that they name: `cols`: used slots come first in each row and -1 marks the unused ones. Slot 0 of block row p names p itself; every other used slot names a block at most 7 away from p, each at most once. The relation is symmetric: p names q exactly when q names p. In every scenario some block row uses all 15 slots. `vals`: the block in row p's slot naming q is the transpose of the block in row q's slot naming p (the self block is symmetric); unused slots hold zeros.
All inputs are finite; a program needn't handle non-finite values.
Results may differ from a plain program's by a relative error of at most 0.0061.
Values may be sent and summed in bfloat16 or wider, within the bound.
No kernel may reach another device: no remote copies, remote signals or barrier semaphores. Data moves between devices by JAX's collectives and lax.ppermute only.
A program may use at most 128 MiB of HBM per device.

v0:
```python
import jax
import jax.numpy as jnp
from jax import lax
from jax.sharding import PartitionSpec as P

REACH = 7


def padded(cells, sides, width):
    for axis, dim in sides:
        count = lax.axis_size(axis)
        ends = count - 1
        head = lax.slice_in_dim(cells, 0, width, axis=dim)
        tail = lax.slice_in_dim(cells, cells.shape[dim] - width, cells.shape[dim], axis=dim)
        cells = jnp.concatenate(
            [
                lax.ppermute(tail, axis, [(i, (i + 1) % count) for i in range(ends)]),
                cells,
                lax.ppermute(head, axis, [((i + 1) % count, i) for i in range(ends)]),
            ],
            axis=dim,
        )
    return cells


def spread(extended, row_cols, row_vals, first):
    row_blocks = row_vals.shape[0]
    block_size = row_vals.shape[2]
    width = extended.shape[1]
    ext_blocks = extended.reshape(-1, block_size, width)
    margin = (ext_blocks.shape[0] - row_blocks) // 2
    local_index = jnp.where(row_cols >= 0, row_cols - first + margin, 0)
    picked = ext_blocks[local_index]
    summed = jnp.einsum("rkab,rkbf->raf", row_vals, picked, preferred_element_type=jnp.float32)
    return summed.reshape(-1, width)


def shards(feats, weight, cols, vals, cotangent):
    first = lax.axis_index(("blk", "rep")) * cols.shape[1]
    rim_rows = REACH * vals.shape[3]
    own = feats[0]
    projected = jnp.dot(own, weight, preferred_element_type=jnp.float32).astype(jnp.bfloat16)
    extended = padded(projected, ((("blk", "rep"), 0),), rim_rows)
    agg = spread(extended, cols[0], vals[0], first)
    sig = jax.nn.sigmoid(agg)
    activ_list = [(agg * sig).astype(jnp.bfloat16)]
    dagg = (cotangent[0].astype(jnp.float32) * sig * (1.0 + agg * (1.0 - sig))).astype(jnp.bfloat16)
    grad_ext = padded(dagg, ((("blk", "rep"), 0),), rim_rows)
    dproj = spread(grad_ext, cols[0], vals[0], first).astype(jnp.bfloat16)
    back = lax.dot_general(
        dproj, weight, (((1,), (1,)), ((), ())), preferred_element_type=jnp.float32
    )
    grad_list = [back.astype(jnp.bfloat16)]
    grads = lax.dot_general(
        own, dproj, (((0,), (0,)), ((), ())), preferred_element_type=jnp.float32
    )
    weight_grad = lax.psum(grads, ("dp", "blk", "rep"))
    return (jnp.stack(activ_list), jnp.stack(grad_list), weight_grad)


def solution(mesh):
    placed = (
        P("dp", ("blk", "rep"), None),
        P(),
        P("dp", ("blk", "rep"), None),
        P("dp", ("blk", "rep"), None, None, None),
        P("dp", ("blk", "rep"), None),
    )
    return jax.shard_map(
        shards,
        mesh=mesh,
        in_specs=placed,
        out_specs=(P("dp", ("blk", "rep"), None), P("dp", ("blk", "rep"), None), P()),
        check_vma=False,
    )
```

profile of v0, /device:TPU:0, one launch (start us, length us, event | category | flops | bytes accessed | tf_op | source)
XLA Modules:
  0.0 287.8 jit_solution(11901660477694064899)
XLA Ops:
  7.2 1.2 copy-done
  8.4 1.7 convolution_convert_fusion.1
  10.1 1.1 fusion.16
  11.2 5.9 %collective-permute-start = (bf16[896,512]{1,0:T(8,128)(2,1)}, bf16[896,512]{1,0:T(8,128)(2,1)}, u32[]{:S(2)}, u32[]{:S(2)}) collective-permute-start(bf16[896,512]{1,0:T(8,128)(2,1)} %get-tuple-element.8), channel_id=1, source_target_pairs={{0,1},{1,2},{2,3},{3,4},{4,5},{5,6},{6,7},{7,8},{8,9},{9,10},{10,1... | collective-permute-start | bytes 2752520 | tf_op jit(solution)/shard_map/ppermute | solution.py:17
  17.1 1.3 collective-permute-start.1
  18.5 17.5 %collective-permute-done = bf16[896,512]{1,0:T(8,128)(2,1)} collective-permute-done((bf16[896,512]{1,0:T(8,128)(2,1)}, bf16[896,512]{1,0:T(8,128)(2,1)}, u32[]{:S(2)}, u32[]{:S(2)}) %collective-permute-start) | collective-permute-done | bytes 917536 | tf_op jit(solution)/shard_map/ppermute | solution.py:17
  36.1 23.3 %collective-permute-done.1 = bf16[896,512]{1,0:T(8,128)(2,1)} collective-permute-done((bf16[896,512]{1,0:T(8,128)(2,1)S(1)}, bf16[896,512]{1,0:T(8,128)(2,1)}, u32[]{:S(2)}, u32[]{:S(2)}) %collective-permute-start.1) | collective-permute-done | bytes 917536 | tf_op jit(solution)/shard_map/ppermute | solution.py:19
  59.3 3.2 %pad_maximum_fusion = bf16[2816,512]{1,0:T(8,128)(2,1)} fusion(bf16[896,512]{1,0:T(8,128)(2,1)} %collective-permute-done.1, bf16[1024,512]{1,0:T(8,128)(2,1)S(1)} %convolution_convert_fusion.1, bf16[896,512]{1,0:T(8,128)(2,1)} %collective-permute-done), kind=kLoop, calls=%fused_computation.6 | loop fusion | flops 8650752 | bytes 5767168 | tf_op jit(solution)/shard_map/concatenate | solution.py:15
  62.6 9.5 %gather_fusion = bf16[120,128,512]{2,1,0:T(8,128)(2,1)} fusion(bf16[22,128,512]{2,1,0:T(8,128)(2,1)} %bitcast.62, s32[1024]{0:T(1024)S(1)} %pad_clamp_fusion), kind=kCustom, calls=%fused_computation | custom fusion | bytes 31457760 | tf_op jit(solution)/shard_map/gather | solution.py:33
  72.1 8.2 %fusion = f32[8,512,128,1]{1,2,3,0:T(8,128)S(1)} fusion(bf16[8,15,128,512]{3,2,1,0:T(8,128)(2,1)} %bitcast.64, bf16[1,8,15,128,128]{4,3,2,1,0:T(8,128)(2,1)} %param.8), kind=kOutput, calls=%fused_computation.2 | convolution fusion | flops 2013265920 | bytes 21757952 | tf_op jit(solution)/shard_map/rkab,rkbf->raf/dot_general | solution.py:34
  80.3 0.8 fusion.5
  81.3 2.5 collective-permute-start.2
  83.8 1.3 collective-permute-start.3
  85.1 18.4 %collective-permute-done.2 = bf16[896,512]{1,0:T(8,128)(2,1)S(1)} collective-permute-done((bf16[896,512]{1,0:T(8,128)(2,1)S(1)}, bf16[896,512]{1,0:T(8,128)(2,1)S(1)}, u32[]{:S(2)}, u32[]{:S(2)}) %collective-permute-start.2) | collective-permute-done | bytes 917536 | tf_op jit(solution)/shard_map/ppermute | solution.py:17
  103.5 23.8 %collective-permute-done.3 = bf16[896,512]{1,0:T(8,128)(2,1)S(1)} collective-permute-done((bf16[896,512]{1,0:T(8,128)(2,1)S(1)}, bf16[896,512]{1,0:T(8,128)(2,1)S(1)}, u32[]{:S(2)}, u32[]{:S(2)}) %collective-permute-start.3) | collective-permute-done | bytes 917536 | tf_op jit(solution)/shard_map/ppermute | solution.py:19
  127.3 1.8 pad_maximum_fusion.1
  129.1 9.5 %gather_fusion.1 = bf16[120,128,512]{2,1,0:T(8,128)(2,1)} fusion(bf16[22,128,512]{2,1,0:T(8,128)(2,1)} %bitcast.61, s32[1024]{0:T(1024)S(1)} %pad_clamp_fusion), kind=kCustom, calls=%fused_computation.1 | custom fusion | bytes 31457760 | tf_op jit(solution)/shard_map/gather | solution.py:33
  138.6 9.0 %bitcast_convert_fusion = bf16[8,512,128]{1,2,0:T(8,128)(2,1)S(1)} fusion(bf16[8,15,128,512]{3,2,1,0:T(8,128)(2,1)} %bitcast.63, bf16[1,8,15,128,128]{4,3,2,1,0:T(8,128)(2,1)} %param.8), kind=kOutput, calls=%fused_computation.11 | convolution fusion | flops 2013790208 | bytes 20709376 | tf_op jit(solution)/shard_map/rkab,rkbf->raf/dot_general | solution.py:34
  147.7 1.0 copy-done.1
  148.6 1.7 convolution_bitcast_fusion
  150.4 1.5 multiply_convert_fusion
  151.9 1.7 fusion.12
  153.6 124.8 %all-reduce.2.cloned.1.call-done = f32[512,512]{0,1:T(8,128)} async-done(((f32[512,512]{0,1:T(8,128)}), f32[512,512]{0,1:T(8,128)}) %all-reduce.2.cloned.1.call-update) | async-done | bytes 1048592 | tf_op jit(solution)/shard_map/psum | solution.py:57
  278.4 2.5 copy.8
  (16 shorter events, 0.3 us)
Async XLA Ops:
  7.2 1.2 copy-start
  7.2 11.2 %copy-start.4 = (s32[1,8,15]{2,1,0:T(8,128)S(1)}, s32[1,8,15]{2,1,0:T(8,128)}, u32[]{:S(2)}) copy-start(s32[1,8,15]{2,1,0:T(8,128)} %param.7) | copy-start | bytes 1444
  7.2 271.2 %all-reduce.2.cloned.1.call-start = ((), (), s32[]{:S(2)}) async-start(), calls=%async_computation | async-start | bytes 2097152 | tf_op jit(solution)/shard_map/psum | solution.py:57
  11.2 24.8 %collective-permute-start = (bf16[896,512]{1,0:T(8,128)(2,1)}, bf16[896,512]{1,0:T(8,128)(2,1)}, u32[]{:S(2)}, u32[]{:S(2)}) collective-permute-start(bf16[896,512]{1,0:T(8,128)(2,1)} %get-tuple-element.8), channel_id=1, source_target_pairs={{0,1},{1,2},{2,3},{3,4},{4,5},{5,6},{6,7},{7,8},{8,9},{9,10},{10,1... | collective-permute-start | bytes 2752520 | tf_op jit(solution)/shard_map/ppermute | solution.py:17
  17.1 42.2 %collective-permute-start.1 = (bf16[896,512]{1,0:T(8,128)(2,1)S(1)}, bf16[896,512]{1,0:T(8,128)(2,1)}, u32[]{:S(2)}, u32[]{:S(2)}) collective-permute-start(bf16[896,512]{1,0:T(8,128)(2,1)S(1)} %get-tuple-element.9), channel_id=1, source_target_pairs={{1,0},{2,1},{3,2},{4,3},{5,4},{6,5},{7,6},{8,7},{9,8},{10,9},{11,1... | collective-permute-start | bytes 2752520 | tf_op jit(solution)/shard_map/ppermute | solution.py:19
  72.1 8.2 %copy-start.3 = (bf16[1,1024,512]{2,1,0:T(8,128)(2,1)S(1)}, bf16[1,1024,512]{2,1,0:T(8,128)(2,1)}, u32[]{:S(2)}) copy-start(bf16[1,1024,512]{2,1,0:T(8,128)(2,1)} %param.9) | copy-start | bytes 3145732
  81.3 22.2 %collective-permute-start.2 = (bf16[896,512]{1,0:T(8,128)(2,1)S(1)}, bf16[896,512]{1,0:T(8,128)(2,1)S(1)}, u32[]{:S(2)}, u32[]{:S(2)}) collective-permute-start(bf16[896,512]{1,0:T(8,128)(2,1)S(1)} %get-tuple-element.6), channel_id=1, source_target_pairs={{0,1},{1,2},{2,3},{3,4},{4,5},{5,6},{6,7},{7,8},{8,9},{9,10},{10,1... | collective-permute-start | bytes 2752520 | tf_op jit(solution)/shard_map/ppermute | solution.py:17
  83.8 43.5 %collective-permute-start.3 = (bf16[896,512]{1,0:T(8,128)(2,1)S(1)}, bf16[896,512]{1,0:T(8,128)(2,1)S(1)}, u32[]{:S(2)}, u32[]{:S(2)}) collective-permute-start(bf16[896,512]{1,0:T(8,128)(2,1)S(1)} %get-tuple-element.7), channel_id=1, source_target_pairs={{1,0},{2,1},{3,2},{4,3},{5,4},{6,5},{7,6},{8,7},{9,8},{10,9},{11,1... | collective-permute-start | bytes 2752520 | tf_op jit(solution)/shard_map/ppermute | solution.py:19
  147.6 1.0 copy-start.1
  150.4 1.5 copy-start.2
  150.4 1.5 copy-start.5
Sparse Core Ops, SparseCore 0:
  150.5 127.8 all-reduce.1
where the time goes:
time: 288 us
  waiting for transfers between devices  208 us (72%)
  local copies, waits for them, and re-layouts  25 us (9%)
  matrix products  22.4 us (8%)
  between operations  14.2 us (5%)
  starting transfers between devices  11 us (4%)
  other arithmetic  7.32 us (3%)
    psum x1, waiting for transfers between devices, shards(): weight_grad = lax.psum(grads, ('dp', 'blk', 'rep'))  125 us
    ppermute x2, waiting for transfers between devices, padded(): lax.ppermute(head, axis, [((i + 1) % count, i) for i in range(ends)])  47.1 us
    ppermute x2, waiting for transfers between devices, padded(): lax.ppermute(tail, axis, [(i, (i + 1) % count) for i in range(ends)])  35.9 us
    gather x2, local copies, waits for them, and re-layouts, spread(): picked = ext_blocks[local_index]  19 us
    dot_general x2, matrix products, spread(): jnp.einsum('rkab,rkbf->raf', row_vals, picked, preferred_element_type=jnp...  17.2 us
    ppermute x2, starting transfers between devices, padded(): lax.ppermute(tail, axis, [(i, (i + 1) % count) for i in range(ends)])  8.42 us
  transfers between devices with their start and end apart: 5, of which 5 were waited for; matrix products, arithmetic and copies ran while one was open for 1% of the time, Pallas kernels for 0%

commit v1 on v0

--- a/solution.py
+++ b/solution.py
@@ -54,7 +54,7 @@
     grads = lax.dot_general(
         own, dproj, (((0,), (0,)), ((), ())), preferred_element_type=jnp.float32
     )
-    weight_grad = lax.psum(grads, ("dp", "blk", "rep"))
+    weight_grad = jnp.sum(lax.all_gather(grads, ("dp", "blk", "rep")), axis=0)
     return (jnp.stack(activ_list), jnp.stack(grad_list), weight_grad)
 
 

time: 288 us -> 394 us (1.37)
  waiting for transfers between devices: 208 us -> 277 us
  local copies, waits for them, and re-layouts: 25 us -> 56.3 us
  other arithmetic: 7.32 us -> 12.7 us
    all_gather x0 -> x1, waiting for transfers between devices: none -> 194 us  [shards(): weight_grad = jnp.sum(lax.all_gather(grads, ('dp', 'blk', 'rep')), axis=0)]
    psum x1 -> x0, waiting for transfers between devices: 125 us -> none  [shards(): weight_grad = lax.psum(grads, ('dp', 'blk', 'rep'))]
    unnamed x13 -> x16, local copies, waits for them, and re-layouts: 4.68 us -> 36 us
    reduce_sum x0 -> x1, other arithmetic: none -> 5.36 us  [shards(): weight_grad = jnp.sum(lax.all_gather(grads, ('dp', 'blk', 'rep')), axis=0)]
where the time goes in v1:
time: 394 us
  waiting for transfers between devices  277 us (70%)
  local copies, waits for them, and re-layouts  56.3 us (14%)
  matrix products  22.4 us (6%)
  between operations  14.2 us (4%)
  other arithmetic  12.7 us (3%)
  starting transfers between devices  11.2 us (3%)
    all_gather x1, waiting for transfers between devices, shards(): weight_grad = jnp.sum(lax.all_gather(grads, ('dp', 'blk', 'rep')), axis=0)  194 us
    ppermute x2, waiting for transfers between devices, padded(): lax.ppermute(head, axis, [((i + 1) % count, i) for i in range(ends)])  47.1 us
    unnamed x16, local copies, waits for them, and re-layouts  36 us
    ppermute x2, waiting for transfers between devices, padded(): lax.ppermute(tail, axis, [(i, (i + 1) % count) for i in range(ends)])  35.7 us
    gather x2, local copies, waits for them, and re-layouts, spread(): picked = ext_blocks[local_index]  19 us
    dot_general x2, matrix products, spread(): jnp.einsum('rkab,rkbf->raf', row_vals, picked, preferred_element_type=jnp...  17.2 us
    ppermute x2, starting transfers between devices, padded(): lax.ppermute(tail, axis, [(i, (i + 1) % count) for i in range(ends)])  8.43 us
  transfers between devices with their start and end apart: 5, of which 5 were waited for; matrix products, arithmetic and copies ran while one was open for 1% of the time, Pallas kernels for 0%

profile of v1, /device:TPU:0, one launch (start us, length us, event | category | flops | bytes accessed | tf_op | source)
XLA Modules:
  0.0 393.6 jit_solution(5051359274626404496)
XLA Ops:
  7.2 1.2 copy-done
  8.4 1.7 convolution_convert_fusion.1
  10.1 1.1 fusion.16
  11.2 5.9 %collective-permute-start = (bf16[896,512]{1,0:T(8,128)(2,1)}, bf16[896,512]{1,0:T(8,128)(2,1)}, u32[]{:S(2)}, u32[]{:S(2)}) collective-permute-start(bf16[896,512]{1,0:T(8,128)(2,1)} %get-tuple-element.8), channel_id=1, source_target_pairs={{0,1},{1,2},{2,3},{3,4},{4,5},{5,6},{6,7},{7,8},{8,9},{9,10},{10,1... | collective-permute-start | bytes 2752520 | tf_op jit(solution)/shard_map/ppermute | solution.py:17
  17.1 1.3 collective-permute-start.1
  18.5 17.5 %collective-permute-done = bf16[896,512]{1,0:T(8,128)(2,1)} collective-permute-done((bf16[896,512]{1,0:T(8,128)(2,1)}, bf16[896,512]{1,0:T(8,128)(2,1)}, u32[]{:S(2)}, u32[]{:S(2)}) %collective-permute-start) | collective-permute-done | bytes 917536 | tf_op jit(solution)/shard_map/ppermute | solution.py:17
  36.0 23.3 %collective-permute-done.1 = bf16[896,512]{1,0:T(8,128)(2,1)} collective-permute-done((bf16[896,512]{1,0:T(8,128)(2,1)S(1)}, bf16[896,512]{1,0:T(8,128)(2,1)}, u32[]{:S(2)}, u32[]{:S(2)}) %collective-permute-start.1) | collective-permute-done | bytes 917536 | tf_op jit(solution)/shard_map/ppermute | solution.py:19
  59.3 3.2 pad_maximum_fusion
  62.6 9.5 %gather_fusion = bf16[120,128,512]{2,1,0:T(8,128)(2,1)} fusion(bf16[22,128,512]{2,1,0:T(8,128)(2,1)} %bitcast.67, s32[1024]{0:T(1024)S(1)} %pad_clamp_fusion), kind=kCustom, calls=%fused_computation | custom fusion | bytes 31457760 | tf_op jit(solution)/shard_map/gather | solution.py:33
  72.1 8.2 %fusion = f32[8,512,128,1]{1,2,3,0:T(8,128)S(1)} fusion(bf16[8,15,128,512]{3,2,1,0:T(8,128)(2,1)} %bitcast.69, bf16[1,8,15,128,128]{4,3,2,1,0:T(8,128)(2,1)} %param.8), kind=kOutput, calls=%fused_computation.3 | convolution fusion | flops 2013265920 | bytes 21757952 | tf_op jit(solution)/shard_map/rkab,rkbf->raf/dot_general | solution.py:34
  81.3 2.5 collective-permute-start.2
  83.8 1.5 collective-permute-start.3
  85.3 18.2 %collective-permute-done.2 = bf16[896,512]{1,0:T(8,128)(2,1)S(1)} collective-permute-done((bf16[896,512]{1,0:T(8,128)(2,1)S(1)}, bf16[896,512]{1,0:T(8,128)(2,1)S(1)}, u32[]{:S(2)}, u32[]{:S(2)}) %collective-permute-start.2) | collective-permute-done | bytes 917536 | tf_op jit(solution)/shard_map/ppermute | solution.py:17
  103.5 23.8 %collective-permute-done.3 = bf16[896,512]{1,0:T(8,128)(2,1)S(1)} collective-permute-done((bf16[896,512]{1,0:T(8,128)(2,1)S(1)}, bf16[896,512]{1,0:T(8,128)(2,1)S(1)}, u32[]{:S(2)}, u32[]{:S(2)}) %collective-permute-start.3) | collective-permute-done | bytes 917536 | tf_op jit(solution)/shard_map/ppermute | solution.py:19
  127.3 1.8 pad_maximum_fusion.1
  129.1 9.5 %gather_fusion.1 = bf16[120,128,512]{2,1,0:T(8,128)(2,1)} fusion(bf16[22,128,512]{2,1,0:T(8,128)(2,1)} %bitcast.66, s32[1024]{0:T(1024)S(1)} %pad_clamp_fusion), kind=kCustom, calls=%fused_computation.1 | custom fusion | bytes 31457760 | tf_op jit(solution)/shard_map/gather | solution.py:33
  138.6 9.0 %bitcast_convert_fusion = bf16[8,512,128]{1,2,0:T(8,128)(2,1)S(1)} fusion(bf16[8,15,128,512]{3,2,1,0:T(8,128)(2,1)} %bitcast.68, bf16[1,8,15,128,128]{4,3,2,1,0:T(8,128)(2,1)} %param.8), kind=kOutput, calls=%fused_computation.12 | convolution fusion | flops 2013790208 | bytes 20709376 | tf_op jit(solution)/shard_map/rkab,rkbf->raf/dot_general | solution.py:34
  148.6 1.7 convolution_bitcast_fusion
  150.4 1.5 multiply_convert_fusion
  151.9 1.7 fusion.12
  153.6 193.9 %all-gather.3.cloned.1.call-done = f32[16384,512]{0,1:T(8,128)} async-done(((f32[512,512]{0,1:T(8,128)}), f32[16384,512]{0,1:T(8,128)}) %all-gather.3.cloned.1.call-update) | async-done | bytes 33554448 | tf_op jit(solution)/shard_map/all_gather | solution.py:57
  347.5 32.5 %copy.11 = f32[64,8,32,512]{3,2,1,0:T(8,128)S(1)} copy(f32[64,8,32,512]{3,1,2,0:T(8,128)} %bitcast.70) | data formatting | bytes 67108864
  380.0 5.4 %bitcast_reduce_fusion = f32[512,512]{0,1:T(8,128)S(1)} fusion(f32[64,8,32,512]{3,2,1,0:T(8,128)S(1)} %copy.11), kind=kLoop, calls=%fused_computation.2 | loop fusion | flops 8126464 | bytes 34603008 | tf_op jit(solution)/shard_map/reduce_sum | solution.py:57
  385.4 1.3 copy.8
  (20 shorter events, 2.1 us)
Async XLA Ops:
  7.2 1.2 copy-start
  7.2 11.2 %copy-start.5 = (s32[1,8,15]{2,1,0:T(8,128)S(1)}, s32[1,8,15]{2,1,0:T(8,128)}, u32[]{:S(2)}) copy-start(s32[1,8,15]{2,1,0:T(8,128)} %param.7) | copy-start | bytes 1444
  7.2 340.3 %all-gather.3.cloned.1.call-start = ((), (), s32[]{:S(2)}) async-start(), calls=%async_computation | async-start | bytes 34603008 | tf_op jit(solution)/shard_map/all_gather | solution.py:57
  11.2 24.8 %collective-permute-start = (bf16[896,512]{1,0:T(8,128)(2,1)}, bf16[896,512]{1,0:T(8,128)(2,1)}, u32[]{:S(2)}, u32[]{:S(2)}) collective-permute-start(bf16[896,512]{1,0:T(8,128)(2,1)} %get-tuple-element.8), channel_id=1, source_target_pairs={{0,1},{1,2},{2,3},{3,4},{4,5},{5,6},{6,7},{7,8},{8,9},{9,10},{10,1... | collective-permute-start | bytes 2752520 | tf_op jit(solution)/shard_map/ppermute | solution.py:17
  17.1 42.2 %collective-permute-start.1 = (bf16[896,512]{1,0:T(8,128)(2,1)S(1)}, bf16[896,512]{1,0:T(8,128)(2,1)}, u32[]{:S(2)}, u32[]{:S(2)}) collective-permute-start(bf16[896,512]{1,0:T(8,128)(2,1)S(1)} %get-tuple-element.9), channel_id=1, source_target_pairs={{1,0},{2,1},{3,2},{4,3},{5,4},{6,5},{7,6},{8,7},{9,8},{10,9},{11,1... | collective-permute-start | bytes 2752520 | tf_op jit(solution)/shard_map/ppermute | solution.py:19
  72.1 8.2 %copy-start.4 = (bf16[1,1024,512]{2,1,0:T(8,128)(2,1)S(1)}, bf16[1,1024,512]{2,1,0:T(8,128)(2,1)}, u32[]{:S(2)}) copy-start(bf16[1,1024,512]{2,1,0:T(8,128)(2,1)} %param.9) | copy-start | bytes 3145732
  81.3 22.2 %collective-permute-start.2 = (bf16[896,512]{1,0:T(8,128)(2,1)S(1)}, bf16[896,512]{1,0:T(8,128)(2,1)S(1)}, u32[]{:S(2)}, u32[]{:S(2)}) collective-permute-start(bf16[896,512]{1,0:T(8,128)(2,1)S(1)} %get-tuple-element.6), channel_id=1, source_target_pairs={{0,1},{1,2},{2,3},{3,4},{4,5},{5,6},{6,7},{7,8},{8,9},{9,10},{10,1... | collective-permute-start | bytes 2752520 | tf_op jit(solution)/shard_map/ppermute | solution.py:17
  83.8 43.5 %collective-permute-start.3 = (bf16[896,512]{1,0:T(8,128)(2,1)S(1)}, bf16[896,512]{1,0:T(8,128)(2,1)S(1)}, u32[]{:S(2)}, u32[]{:S(2)}) collective-permute-start(bf16[896,512]{1,0:T(8,128)(2,1)S(1)} %get-tuple-element.7), channel_id=1, source_target_pairs={{1,0},{2,1},{3,2},{4,3},{5,4},{6,5},{7,6},{8,7},{9,8},{10,9},{11,1... | collective-permute-start | bytes 2752520 | tf_op jit(solution)/shard_map/ppermute | solution.py:19
  147.6 1.0 copy-start.2
  150.4 1.6 copy-start.3
  150.4 1.5 copy-start.6
  380.0 6.7 %copy-start.1 = (bf16[1,1024,512]{2,1,0:T(8,128)(2,1)S(1)}, bf16[1,1024,512]{2,1,0:T(8,128)(2,1)}, u32[]{:S(2)}) copy-start(bf16[1,1024,512]{2,1,0:T(8,128)(2,1)} %param.5) | copy-start | bytes 3145732
Sparse Core Ops, SparseCore 0:
  150.5 196.9 all-gather.2
